TPU v7x, 32 devices: a whole 2x2x4 slice. The times are simulated.
32 devices in a mesh: facet: 8 (over z, x), strip: 4 (over y, core).
Axes of the slice: x: 2, y: 2, z: 4, core: 2. Of those that a mesh axis runs over, the one named last changes fastest.
Arguments:
- facets: bfloat16 [8, 2, 512, 8192], P('facet', None, None, 'strip'), may hold values from -6 to 6
- offsets: int32 [4], replicated, may hold values from 0 to 32767
- visibilities: float32 [2, 512, 2048], P(None, 'strip', 'facet'), may hold values from -24 to 24
- weights: float32 [512, 2048], P('strip', 'facet'), may hold values from 0.1 to 1
- mask: int32 [512, 2048], P('strip', 'facet'), may hold values 0 or 1
Outputs:
- facet_update: bfloat16 [8, 2, 512, 8192], P('facet', None, None, 'strip')
Inputs may be any that keep to these rules, and one draw needn't show every extreme that they name: `mask`: 1 where the cell holds a sampled visibility.
All inputs are finite; a program needn't handle non-finite values. No bound on the sum of `mask` on one device may be relied on, other than what follows from the above.
Results may differ from a plain program's by a relative error of at most 0.0058.
Values may be sent and summed in bfloat16 or wider, within the bound.
No kernel may reach another device: no remote copies, remote signals or barrier semaphores. Data moves between devices by JAX's collectives and lax.ppermute only.
A program may use at most 128 MiB of HBM per device.

v0:
```python
import math
import jax
import jax.numpy as jnp
from jax import lax
from jax.sharding import PartitionSpec as P

NG = 32768
XM = 8192
SG = 512
NSUB = 4
FROWS = 4


def residue_angle(count):
    return count.astype(jnp.float32) * (2.0 * math.pi / NG)


def dft_kernel(rows):
    positions = jnp.arange(rows, dtype=jnp.int32)
    cells = jnp.arange(SG, dtype=jnp.int32)
    angle = residue_angle(positions[:, None] * cells[None, :] % NG)
    return jnp.concatenate([jnp.cos(angle), jnp.sin(angle)], axis=1).astype(jnp.bfloat16)


def row_angles(start, rows, offsets):
    positions = start + jnp.arange(rows, dtype=jnp.int32)
    return residue_angle(offsets[:, None] * positions[None, :] % NG)


def column_angles(facet_index, offsets):
    centre = (facet_index % FROWS * XM + NG // 2) % NG
    cells = jnp.arange(SG, dtype=jnp.int32)
    return residue_angle((cells[None, :] * centre % NG + offsets[:, None] * centre % NG) % NG)


def forward(data, start, facet_index, offsets, kernel_table):
    columns = data.shape[1]
    rows = data.shape[2]
    phi = row_angles(start, rows, offsets)[:, None, :]
    cos_phi = jnp.cos(phi)
    sin_phi = jnp.sin(phi)
    real_part = data[0].astype(jnp.float32)[None]
    imag_part = data[1].astype(jnp.float32)[None]
    twisted = jnp.stack(
        [real_part * cos_phi + imag_part * sin_phi, imag_part * cos_phi - real_part * sin_phi],
        axis=1,
    ).astype(jnp.bfloat16)
    spectra = jnp.dot(twisted.reshape(-1, rows), kernel_table, preferred_element_type=jnp.float32)
    spectra = spectra.reshape(NSUB, 2, columns, 2, SG)
    spectrum_real = spectra[:, 0, :, 0] + spectra[:, 1, :, 1]
    spectrum_imag = spectra[:, 1, :, 0] - spectra[:, 0, :, 1]
    psi = column_angles(facet_index, offsets)[:, None, :]
    cos_psi = jnp.cos(psi)
    sin_psi = jnp.sin(psi)
    scale = 1.0 / math.sqrt(XM)
    result_real = (spectrum_real * cos_psi + spectrum_imag * sin_psi) * scale
    result_imag = (spectrum_imag * cos_psi - spectrum_real * sin_psi) * scale
    stacked = jnp.stack([result_real, result_imag])
    return stacked.transpose(0, 2, 1, 3).reshape(2, columns, NSUB * SG)


def adjoint(residual, start, facet_index, offsets, kernel_table):
    columns = residual.shape[1]
    rows = kernel_table.shape[0]
    values = residual.astype(jnp.float32).reshape(2, columns, NSUB, SG).transpose(0, 2, 1, 3)
    psi = column_angles(facet_index, offsets)[:, None, :]
    cos_psi = jnp.cos(psi)
    sin_psi = jnp.sin(psi)
    first = values[0] * cos_psi - values[1] * sin_psi
    second = values[1] * cos_psi + values[0] * sin_psi
    untwisted = jnp.stack([first, second], axis=1).astype(jnp.bfloat16)
    images = jnp.einsum(
        "mj,xpj->pmx",
        untwisted.reshape(-1, SG),
        kernel_table.reshape(rows, 2, SG),
        preferred_element_type=jnp.float32,
    )
    images = images.reshape(2, NSUB, 2, columns, rows)
    image_real = images[0, :, 0] - images[1, :, 1]
    image_imag = images[0, :, 1] + images[1, :, 0]
    phi = row_angles(start, rows, offsets)[:, None, :]
    cos_phi = jnp.cos(phi)
    sin_phi = jnp.sin(phi)
    scale = 1.0 / math.sqrt(XM)
    total_real = jnp.sum(image_real * cos_phi - image_imag * sin_phi, axis=0) * scale
    total_imag = jnp.sum(image_imag * cos_phi + image_real * sin_phi, axis=0) * scale
    return jnp.stack([total_real, total_imag])


def weigh(model, visibilities, weights, mask):
    factor = weights * mask.astype(jnp.float32)
    return (factor[None] * (visibilities - model)).astype(jnp.bfloat16)


def on_device(facets, offsets, visibilities, weights, mask):
    facet_index = lax.axis_index("facet")
    regrouped = lax.all_to_all(facets[0], "strip", split_axis=1, concat_axis=2, tiled=True)
    kernel_table = dft_kernel(regrouped.shape[2])
    contribution = forward(regrouped, 0, facet_index, offsets, kernel_table)
    model = lax.psum_scatter(contribution, "facet", scatter_dimension=2, tiled=True)
    residual = weigh(model, visibilities, weights, mask)
    gathered = lax.all_gather(residual, "facet", axis=2, tiled=True)
    update = adjoint(gathered, 0, facet_index, offsets, kernel_table).astype(jnp.bfloat16)
    result = lax.all_to_all(update, "strip", split_axis=2, concat_axis=1, tiled=True)
    return result[None]


def solution(mesh):
    placed = (
        P("facet", None, None, "strip"),
        P(),
        P(None, "strip", "facet"),
        P("strip", "facet"),
        P("strip", "facet"),
    )
    return jax.shard_map(
        on_device,
        mesh=mesh,
        in_specs=placed,
        out_specs=P("facet", None, None, "strip"),
        check_vma=False,
    )
```

profile of v0, /device:TPU:0, one launch (start us, length us, event | category | flops | bytes accessed | tf_op | source)
XLA Modules:
  0.0 451.6 jit_solution(7619882456607674424)
XLA Ops:
  6.5 8.5 %copy.105 = bf16[1,2,512,2048]{3,1,2,0:T(2,128)(2,1)} copy(bf16[1,2,512,2048]{3,2,1,0:T(8,128)(2,1)} %param.5) | data formatting | bytes 8388608 | tf_op args[0]
  15.1 4.9 %all-to-all-start = ((bf16[2,512,2048]{2,0,1:T(2,128)(2,1)}), bf16[2,512,2048]{2,0,1:T(2,128)(2,1)}, u32[]{:S(2)}, u32[]{:S(2)}) async-start(bf16[2,512,2048]{2,0,1:T(2,128)(2,1)} %bitcast.137), calls=%async_computation | async-start | bytes 8388608 | tf_op jit(solution)/shard_map/all_to_all | solution.py:97
  19.9 0.2 reduce-scatter.2.cloned.1.call-start
  20.2 67.2 %sine_convert_fusion = (bf16[8192,512]{0,1:T(8,128)(2,1)}, bf16[8192,512]{0,1:T(8,128)(2,1)}) fusion(), kind=kLoop, calls=%fused_computation.31 | loop fusion | flops 67108864 | bytes 16777216 | tf_op jit(solution)/shard_map/convert.11
  87.6 13.7 %pad_maximum_fusion = bf16[8192,1024]{0,1:T(8,128)(2,1)} fusion(bf16[8192,512]{0,1:T(8,128)(2,1)} %get-tuple-element.19, bf16[8192,512]{0,1:T(8,128)(2,1)} %get-tuple-element.20), kind=kLoop, calls=%fused_computation.28 | loop fusion | flops 33554432 | bytes 33554432 | tf_op jit(solution)/shard_map/concatenate | solution.py:22
  101.3 1.2 fusion.32
  102.5 4.1 copy.77
  106.6 4.4 slice_convert_fusion.1
  111.0 5.3 %copy.78 = f32[1,128,4,2048]{1,3,2,0:T(8,128)} copy(f32[1,128,4,2048]{3,1,2,0:T(8,128)} %get-tuple-element.11) | data formatting | bytes 8388608 | tf_op jit(solution)/shard_map/convert_element_type | solution.py:42
  116.3 5.6 %copy.79 = f32[128,8192]{1,0:T(8,128)} copy(f32[128,8192]{0,1:T(8,128)} %bitcast.138) | data formatting | bytes 8388608 | tf_op jit(solution)/shard_map/convert_element_type | solution.py:42
  121.9 5.3 %copy.80 = f32[1,128,4,2048]{1,3,2,0:T(8,128)} copy(f32[1,128,4,2048]{3,1,2,0:T(8,128)} %get-tuple-element.12) | data formatting | bytes 8388608 | tf_op jit(solution)/shard_map/convert_element_type | solution.py:43
  127.3 5.6 %copy.81 = f32[128,8192]{1,0:T(8,128)} copy(f32[128,8192]{0,1:T(8,128)} %bitcast.139) | data formatting | bytes 8388608 | tf_op jit(solution)/shard_map/convert_element_type | solution.py:43
  132.9 6.5 %add_convert_fusion = (bf16[4,1,128,8192]{3,2,1,0:T(8,128)(2,1)S(1)}, bf16[4,1,128,8192]{3,2,1,0:T(8,128)(2,1)S(1)}) fusion(f32[4,8192]{1,0:T(4,128)S(1)} %get-tuple-element.18, f32[128,8192]{1,0:T(8,128)} %copy.81, f32[4,8192]{1,0:T(4,128)S(1)} %get-tuple-element.17, f32[128,8192]{1,0:T(8,128)} %copy.79), kind=kLoop, calls=%fused_computation.36 | loop fusion | flops 33554432 | bytes 25427968 | tf_op jit(solution)/shard_map/convert.12
  139.4 21.8 %fusion.14 = f32[4,2,128,2,512]{4,2,3,1,0:T(8,128)S(1)} fusion(bf16[2,512,8192,1,1]{2,1,0,4,3:T(8,128)(2,1)} %bitcast.136, bf16[4,1,128,8192]{3,2,1,0:T(8,128)(2,1)S(1)} %get-tuple-element.8, bf16[4,1,128,8192]{3,2,1,0:T(8,128)(2,1)S(1)} %get-tuple-element.7), kind=kOutput, calls=%fused_computation.25 | convolution fusion | flops 17213423616 | bytes 37748736 | tf_op jit(solution)/shard_map/dot_general | solution.py:48
  161.2 0.7 add_multiply_fusion
  161.9 0.2 maximum_bitcast_fusion.2
  162.1 1.8 copy.84
  164.0 0.3 all-gather.2.cloned.1.call-start
  164.5 70.9 %reduce-scatter.2.cloned.1.call-done = f32[2,128,256]{1,2,0:T(8,128)} async-done(((f32[2,128,2048]{1,2,0:T(8,128)}), f32[2,128,256]{1,2,0:T(8,128)}) %reduce-scatter.2.cloned.1.call-update) | async-done | bytes 262160 | tf_op jit(solution)/shard_map/reduce_scatter | solution.py:100
  235.4 1.6 multiply_convert_fusion.2
  237.0 68.4 %sine_convert_fusion.1 = (bf16[8192,1,512]{2,0,1:T(8,128)(2,1)}, bf16[8192,1,512]{2,0,1:T(8,128)(2,1)}) fusion(), kind=kLoop, calls=%fused_computation.37 | loop fusion | flops 67108864 | bytes 16777216 | tf_op jit(solution)/shard_map/convert.15
  305.4 1.5 copy.86
  306.9 0.3 subtract_convert_fusion.1
  307.3 31.5 %fusion.10 = f32[8192,2,1024]{0,2,1:T(8,128)} fusion(bf16[1024,512,1]{1,0,2:T(8,128)(2,1)S(1)} %bitcast.144, bf16[8192,1,512]{2,0,1:T(8,128)(2,1)} %get-tuple-element.21, bf16[8192,1,512]{2,0,1:T(8,128)(2,1)} %get-tuple-element.22), kind=kOutput, calls=%fused_computation.20 | convolution fusion | flops 17188257792 | bytes 84934656 | tf_op jit(solution)/shard_map/mj,xpj->pmx/dot_general | solution.py:72
  338.8 26.7 %subtract_reduce_fusion = (f32[128,8192]{1,0:T(8,128)}, f32[128,8192]{1,0:T(8,128)}) fusion(f32[4,8192]{1,0:T(4,128)S(1)} %get-tuple-element.18, f32[4,8192]{1,0:T(4,128)S(1)} %get-tuple-element.17, f32[2,4,2,128,8192]{4,3,2,1,0:T(8,128)} %bitcast.25), kind=kLoop, calls=%fused_computation.30 | loop fusion | flops 39845888 | bytes 75759616 | tf_op jit(solution)/shard_map/reduce_sum | solution.py:85
  365.5 2.6 fusion.23
  368.0 2.6 fusion.24
  370.6 2.4 pad_maximum_fusion.1
  373.0 11.1 %copy.93 = bf16[2,128,8192]{1,0,2:T(2,128)(2,1)} copy(bf16[2,128,8192]{2,1,0:T(8,128)(2,1)} %pad_maximum_fusion.1) | data formatting | bytes 8388608 | tf_op jit(solution)/shard_map/stack | solution.py:87
  384.1 51.9 %all_to_all.30 = bf16[2,128,8192]{1,0,2:T(2,128)(2,1)S(1)} all-to-all(bf16[2,128,8192]{1,0,2:T(2,128)(2,1)} %copy.93), channel_id=1, replica_groups=mesh['facet'=8,'strip'=4] {'strip'}, dimensions={2} | all-to-all | bytes 8388608 | tf_op jit(solution)/shard_map/all_to_all | solution.py:104
  436.0 2.5 copy.94
  438.5 6.2 %copy.95 = bf16[2,4,128,2048]{3,2,1,0:T(8,128)(2,1)} copy(bf16[2,4,128,2048]{2,3,1,0:T(8,128)(2,1)} %bitcast.140) | data formatting | bytes 8388608 | tf_op jit(solution)/shard_map/all_to_all | solution.py:104
  (19 shorter events, 0.6 us)
Async XLA Ops:
  6.5 80.9 %copy-start.3 = (s32[4]{0:T(128)S(1)}, s32[4]{0:T(128)}, u32[]{:S(2)}) copy-start(s32[4]{0:T(128)} %param.6) | copy-start | bytes 52
  15.1 87.5 %all-to-all-start = ((bf16[2,512,2048]{2,0,1:T(2,128)(2,1)}), bf16[2,512,2048]{2,0,1:T(2,128)(2,1)}, u32[]{:S(2)}, u32[]{:S(2)}) async-start(bf16[2,512,2048]{2,0,1:T(2,128)(2,1)} %bitcast.137), calls=%async_computation | async-start | bytes 8388608 | tf_op jit(solution)/shard_map/all_to_all | solution.py:97
  19.9 215.4 %reduce-scatter.2.cloned.1.call-start = ((), (), s32[]{:S(2)}) async-start(), calls=%async_computation.3 | async-start | bytes 2359296 | tf_op jit(solution)/shard_map/reduce_scatter | solution.py:100
  161.2 3.0 copy-start.1
  161.2 3.0 copy-start.2
  161.2 3.1 copy-start
  164.0 141.5 %all-gather.2.cloned.1.call-start = ((), (), s32[]{:S(2)}) async-start(), calls=%async_computation.4 | async-start | bytes 1179648 | tf_op jit(solution)/shard_map/all_gather | solution.py:102
Sparse Core Ops, SparseCore 0:
  164.1 71.2 reduce-scatter.1
  237.6 39.2 all-gather.1
where the time goes:
time: 453 us; the launch traced here: 452 us
  other arithmetic  199 us (44%)
  waiting for transfers between devices  70.9 us (16%)
  local copies, waits for them, and re-layouts  57.8 us (13%)
  matrix products  53.2 us (12%)
  blocking collectives  51.9 us (11%)
  between operations  13.6 us (3%)
  starting transfers between devices  5.36 us (1%)
    another operation x4, other arithmetic  142 us
    reduce_scatter x1, waiting for transfers between devices, on_device(): lax.psum_scatter(contribution, 'facet', scatter_dimension=2, tiled=True)  70.9 us
    all_to_all x1, blocking collectives, on_device(): lax.all_to_all(update, 'strip', split_axis=2, concat_axis=1, tiled=True)  51.9 us
    dot_general x1, matrix products, adjoint(): jnp.einsum('mj,xpj->pmx', untwisted.reshape(-1, SG), kernel_table.reshape...  31.5 us
    reduce_sum x1, other arithmetic, adjoint(): jnp.sum(image_real * cos_phi - image_imag * sin_phi, axis=0) * scale  26.7 us
    dot_general x1, matrix products, forward(): jnp.dot(twisted.reshape(-1, rows), kernel_table, preferred_element_type=j...  21.8 us
    concatenate x1, other arithmetic, dft_kernel(): jnp.concatenate([jnp.cos(angle), jnp.sin(angle)], axis=1)  13.7 us
    another operation x1, local copies, waits for them, and re-layouts, adjoint(): return jnp.stack([total_real, total_imag])  11.1 us
  transfers between devices with their start and end apart: 3, of which 1 were waited for; matrix products, arithmetic and copies ran while one was open for 33% of the time, Pallas kernels for 0%

commit v1 on v0

--- a/solution.py
+++ b/solution.py
@@ -101,7 +101,9 @@
     residual = weigh(model, visibilities, weights, mask)
     gathered = lax.all_gather(residual, "facet", axis=2, tiled=True)
     update = adjoint(gathered, 0, facet_index, offsets, kernel_table).astype(jnp.bfloat16)
-    result = lax.all_to_all(update, "strip", split_axis=2, concat_axis=1, tiled=True)
+    pieces = jnp.split(update, lax.axis_size("strip"), axis=2)
+    got = lax.all_to_all(jnp.stack(pieces), "strip", 0, 0)
+    result = jnp.concatenate(got, axis=1)
     return result[None]
 
 

time: 453 us -> 431 us (0.951)
  local copies, waits for them, and re-layouts: 57.8 us -> 41.1 us
    another operation x1 -> x0, local copies, waits for them, and re-layouts: 11.1 us -> none  [adjoint(): return jnp.stack([total_real, total_imag])]
    all_to_all x2 -> x1, local copies, waits for them, and re-layouts: 8.68 us -> 2.32 us  [on_device(): got = lax.all_to_all(jnp.stack(pieces), 'strip', 0, 0)]
    another operation x5 -> x6, other arithmetic: 145 us -> 143 us
    unnamed x10 -> x12, local copies, waits for them, and re-layouts: 8.67 us -> 9.38 us
  transfers between devices with their start and end apart: 3 -> 3, of which waited for: 1 -> 1; matrix products, arithmetic and copies ran while one was open for 33% -> 35% of each run, Pallas kernels for 0% -> 0%
where the time goes in v1:
time: 431 us; the launch traced here: 430 us
  other arithmetic  195 us (45%)
  waiting for transfers between devices  70.8 us (16%)
  matrix products  53.2 us (12%)
  blocking collectives  50.7 us (12%)
  local copies, waits for them, and re-layouts  41.1 us (10%)
  between operations  13.7 us (3%)
  starting transfers between devices  5.35 us (1%)
    another operation x4, other arithmetic  142 us
    reduce_scatter x1, waiting for transfers between devices, on_device(): lax.psum_scatter(contribution, 'facet', scatter_dimension=2, tiled=True)  70.8 us
    all_to_all x1, blocking collectives, on_device(): got = lax.all_to_all(jnp.stack(pieces), 'strip', 0, 0)  50.7 us
    dot_general x1, matrix products, adjoint(): jnp.einsum('mj,xpj->pmx', untwisted.reshape(-1, SG), kernel_table.reshape...  31.5 us
    reduce_sum x1, other arithmetic, adjoint(): jnp.sum(image_real * cos_phi - image_imag * sin_phi, axis=0) * scale  26.7 us
    dot_general x1, matrix products, forward(): jnp.dot(twisted.reshape(-1, rows), kernel_table, preferred_element_type=j...  21.8 us
    concatenate x1, other arithmetic, dft_kernel(): jnp.concatenate([jnp.cos(angle), jnp.sin(angle)], axis=1)  13.7 us
    convert_element_type x2, local copies, waits for them, and re-layouts, forward(): real_part = data[0].astype(jnp.float32)[None]  11 us
  transfers between devices with their start and end apart: 3, of which 1 were waited for; matrix products, arithmetic and copies ran while one was open for 35% of the time, Pallas kernels for 0%

profile of v1, /device:TPU:0, one launch (start us, length us, event | category | flops | bytes accessed | tf_op | source)
XLA Modules:
  0.0 430.1 jit_solution(9793509027000645802)
XLA Ops:
  6.5 8.5 %copy.97 = bf16[1,2,512,2048]{3,1,2,0:T(2,128)(2,1)} copy(bf16[1,2,512,2048]{3,2,1,0:T(8,128)(2,1)} %param.5) | data formatting | bytes 8388608 | tf_op args[0]
  15.0 4.9 %all-to-all-start = ((bf16[2,512,2048]{2,0,1:T(2,128)(2,1)}), bf16[2,512,2048]{2,0,1:T(2,128)(2,1)}, u32[]{:S(2)}, u32[]{:S(2)}) async-start(bf16[2,512,2048]{2,0,1:T(2,128)(2,1)} %bitcast.126), calls=%async_computation | async-start | bytes 8388608 | tf_op jit(solution)/shard_map/all_to_all | solution.py:97
  19.9 0.2 reduce-scatter.2.cloned.1.call-start
  20.2 67.2 %sine_convert_fusion = (bf16[8192,512]{0,1:T(8,128)(2,1)}, bf16[8192,512]{0,1:T(8,128)(2,1)}) fusion(), kind=kLoop, calls=%fused_computation.29 | loop fusion | flops 67108864 | bytes 16777216 | tf_op jit(solution)/shard_map/convert.11
  87.6 13.7 %pad_maximum_fusion = bf16[8192,1024]{0,1:T(8,128)(2,1)} fusion(bf16[8192,512]{0,1:T(8,128)(2,1)} %get-tuple-element.23, bf16[8192,512]{0,1:T(8,128)(2,1)} %get-tuple-element.24), kind=kLoop, calls=%fused_computation.26 | loop fusion | flops 33554432 | bytes 33554432 | tf_op jit(solution)/shard_map/concatenate | solution.py:22
  101.3 1.2 fusion.38
  102.5 4.1 copy.75
  106.6 4.4 %slice_convert_fusion.1 = (f32[1,128,4,2048]{3,1,2,0:T(8,128)}, f32[1,128,4,2048]{3,1,2,0:T(8,128)}) fusion(bf16[2,128,4,2048]{3,1,2,0:T(8,128)(2,1)S(1)} %bitcast.124), kind=kLoop, calls=%fused_computation.54 | loop fusion | flops 2097152 | bytes 12582912 | tf_op jit(solution)/shard_map/convert_element_type | solution.py:42
  111.0 5.4 %copy.76 = f32[1,128,4,2048]{1,3,2,0:T(8,128)} copy(f32[1,128,4,2048]{3,1,2,0:T(8,128)} %get-tuple-element.15) | data formatting | bytes 8388608 | tf_op jit(solution)/shard_map/convert_element_type | solution.py:42
  116.3 5.7 %copy.77 = f32[128,8192]{1,0:T(8,128)} copy(f32[128,8192]{0,1:T(8,128)} %bitcast.127) | data formatting | bytes 8388608 | tf_op jit(solution)/shard_map/convert_element_type | solution.py:42
  122.0 5.3 %copy.78 = f32[1,128,4,2048]{1,3,2,0:T(8,128)} copy(f32[1,128,4,2048]{3,1,2,0:T(8,128)} %get-tuple-element.16) | data formatting | bytes 8388608 | tf_op jit(solution)/shard_map/convert_element_type | solution.py:43
  127.3 5.6 %copy.79 = f32[128,8192]{1,0:T(8,128)} copy(f32[128,8192]{0,1:T(8,128)} %bitcast.128) | data formatting | bytes 8388608 | tf_op jit(solution)/shard_map/convert_element_type | solution.py:43
  133.0 6.5 %add_convert_fusion = (bf16[4,1,128,8192]{3,2,1,0:T(8,128)(2,1)S(1)}, bf16[4,1,128,8192]{3,2,1,0:T(8,128)(2,1)S(1)}) fusion(f32[4,8192]{1,0:T(4,128)S(1)} %get-tuple-element.22, f32[128,8192]{1,0:T(8,128)} %copy.79, f32[4,8192]{1,0:T(4,128)S(1)} %get-tuple-element.21, f32[128,8192]{1,0:T(8,128)} %copy.77), kind=kLoop, calls=%fused_computation.34 | loop fusion | flops 33554432 | bytes 25427968 | tf_op jit(solution)/shard_map/convert.12
  139.5 21.8 %fusion.13 = f32[4,2,128,2,512]{4,2,3,1,0:T(8,128)S(1)} fusion(bf16[2,512,8192,1,1]{2,1,0,4,3:T(8,128)(2,1)} %bitcast.125, bf16[4,1,128,8192]{3,2,1,0:T(8,128)(2,1)S(1)} %get-tuple-element.8, bf16[4,1,128,8192]{3,2,1,0:T(8,128)(2,1)S(1)} %get-tuple-element.7), kind=kOutput, calls=%fused_computation.23 | convolution fusion | flops 17213423616 | bytes 37748736 | tf_op jit(solution)/shard_map/dot_general | solution.py:48
  161.3 0.7 add_multiply_fusion
  162.0 0.2 maximum_bitcast_fusion.2
  162.2 1.8 copy.82
  164.0 0.3 all-gather.2.cloned.1.call-start
  164.6 70.8 %reduce-scatter.2.cloned.1.call-done = f32[2,128,256]{1,2,0:T(8,128)} async-done(((f32[2,128,2048]{1,2,0:T(8,128)}), f32[2,128,256]{1,2,0:T(8,128)}) %reduce-scatter.2.cloned.1.call-update) | async-done | bytes 262160 | tf_op jit(solution)/shard_map/reduce_scatter | solution.py:100
  235.4 1.6 multiply_convert_fusion.2
  237.0 68.3 %sine_convert_fusion.1 = (bf16[8192,1,512]{2,0,1:T(8,128)(2,1)}, bf16[8192,1,512]{2,0,1:T(8,128)(2,1)}) fusion(), kind=kLoop, calls=%fused_computation.35 | loop fusion | flops 67108864 | bytes 16777216 | tf_op jit(solution)/shard_map/convert.15
  305.4 1.5 copy.84
  306.9 0.3 subtract_convert_fusion.1
  307.3 31.5 %fusion.9 = f32[8192,2,1024]{0,2,1:T(8,128)} fusion(bf16[1024,512,1]{1,0,2:T(8,128)(2,1)S(1)} %bitcast.132, bf16[8192,1,512]{2,0,1:T(8,128)(2,1)} %get-tuple-element.25, bf16[8192,1,512]{2,0,1:T(8,128)(2,1)} %get-tuple-element.26), kind=kOutput, calls=%fused_computation.18 | convolution fusion | flops 17188257792 | bytes 84934656 | tf_op jit(solution)/shard_map/mj,xpj->pmx/dot_general | solution.py:72
  338.8 26.7 %subtract_reduce_fusion = (f32[128,8192]{1,0:T(8,128)}, f32[128,8192]{1,0:T(8,128)}) fusion(f32[4,8192]{1,0:T(4,128)S(1)} %get-tuple-element.22, f32[4,8192]{1,0:T(4,128)S(1)} %get-tuple-element.21, f32[2,4,2,128,8192]{4,3,2,1,0:T(8,128)} %bitcast.25), kind=kLoop, calls=%fused_computation.28 | loop fusion | flops 39845888 | bytes 75759616 | tf_op jit(solution)/shard_map/reduce_sum | solution.py:85
  365.4 2.7 fusion.22
  368.2 0.7 copy-done
  368.9 0.4 fusion.23
  369.3 0.3 fusion.27
  369.6 0.6 pad_maximum_fusion.1
  370.2 50.7 %all_to_all.20 = bf16[4,2,128,2048]{3,2,1,0:T(8,128)(2,1)S(1)} all-to-all(bf16[4,2,128,2048]{3,2,1,0:T(8,128)(2,1)S(1)} %pad_maximum_fusion.1), channel_id=1, replica_groups=mesh['facet'=8,'strip'=4] {'strip'}, dimensions={0} | all-to-all | bytes 8388608 | tf_op jit(solution)/shard_map/all_to_all | solution.py:105
  420.9 2.3 copy.89
  (20 shorter events, 0.6 us)
Async XLA Ops:
  15.0 87.5 %all-to-all-start = ((bf16[2,512,2048]{2,0,1:T(2,128)(2,1)}), bf16[2,512,2048]{2,0,1:T(2,128)(2,1)}, u32[]{:S(2)}, u32[]{:S(2)}) async-start(bf16[2,512,2048]{2,0,1:T(2,128)(2,1)} %bitcast.126), calls=%async_computation | async-start | bytes 8388608 | tf_op jit(solution)/shard_map/all_to_all | solution.py:97
  19.9 215.5 %reduce-scatter.2.cloned.1.call-start = ((), (), s32[]{:S(2)}) async-start(), calls=%async_computation.3 | async-start | bytes 2359296 | tf_op jit(solution)/shard_map/reduce_scatter | solution.py:100
  20.2 67.2 %copy-start.4 = (s32[4]{0:T(128)S(1)}, s32[4]{0:T(128)}, u32[]{:S(2)}) copy-start(s32[4]{0:T(128)} %param.6) | copy-start | bytes 52
  161.3 3.0 copy-start.2
  161.3 3.0 copy-start.3
  161.3 3.1 copy-start.1
  164.0 141.3 %all-gather.2.cloned.1.call-start = ((), (), s32[]{:S(2)}) async-start(), calls=%async_computation.4 | async-start | bytes 1179648 | tf_op jit(solution)/shard_map/all_gather | solution.py:102
  365.4 3.4 copy-start
Sparse Core Ops, SparseCore 0:
  164.2 71.1 reduce-scatter.1
  237.6 39.2 all-gather.1
